TPU v7x, 32 devices: a whole 2x2x4 slice. The times are simulated.
32 devices in a mesh: slab: 8 (over z, x), row: 4 (over y, core).
Axes of the slice: x: 2, y: 2, z: 4, core: 2. Of those that a mesh axis runs over, the one named last changes fastest.
Arguments:
- edge_weights: int32 [3, 16, 32, 512], P(None, 'slab', 'row'), may hold values from 1 to 15
- seeds: int32 [16, 32, 512], P('slab', 'row'), may hold values from -8 to 7
- supervoxel: int32 [16, 32, 512], P('slab', 'row'), may hold values from 0 to 127
- coarse_blocks: float32 [4, 1024, 1024], P('row', 'slab'), as said below
Outputs:
- potentials: float32 [8, 16, 32, 512], P(None, 'slab', 'row')
Inputs may be any that keep to these rules, and one draw needn't show every extreme that they name: `seeds`: a negative value marks an unseeded voxel. `coarse_blocks`: the entries named by dc lie between 0.6 and 1.2 times 2 * 8 * 4.
All inputs are finite; a program needn't handle non-finite values.
Results may differ from a plain program's by a relative error of at most 0.00024.
Values sent between devices are 32-bit elements; how exact they have to be, the bound alone decides.
No kernel may reach another device: no remote copies, remote signals or barrier semaphores. Data moves between devices by JAX's collectives and lax.ppermute only.
A program may use at most 64 MiB of HBM per device.

v0:
```python
import math
import jax
import jax.numpy as jnp
from jax import lax
from jax.sharding import PartitionSpec as P

LABELS = 8
CZ = 2
CY = 8
NX = 512
CC = 128
CYCLES = 2
prior_mass = 0.25
seed_weight = 4.0
smooth_step = 0.8
coarse_step = 0.7
weight_unit = 0.125


def padded(cells, sides, width):
    for axis, dim in sides:
        count = lax.axis_size(axis)
        ends = count - 1
        head = lax.slice_in_dim(cells, 0, width, axis=dim)
        tail = lax.slice_in_dim(cells, cells.shape[dim] - width, cells.shape[dim], axis=dim)
        cells = jnp.concatenate(
            [
                lax.ppermute(tail, axis, [(i, (i + 1) % count) for i in range(ends)]),
                cells,
                lax.ppermute(head, axis, [((i + 1) % count, i) for i in range(ends)]),
            ],
            axis=dim,
        )
    return cells


def shifted(block, axis, distance):
    devices = range(lax.axis_size(axis))
    route = [(i - distance, i) for i in devices if i - distance in devices]
    return lax.ppermute(block, axis, route)


def lower_x(a):
    return jnp.pad(a[..., :-1], [(0, 0)] * (a.ndim - 1) + [(1, 0)])


def upper_x(a):
    return jnp.pad(a[..., 1:], [(0, 0)] * (a.ndim - 1) + [(0, 1)])


def crop(a, margin):
    return a[..., margin : a.shape[-3] - margin, margin : a.shape[-2] - margin, :]


def rim_one(field):
    return padded(field, (("slab", 1), ("row", 2)), 1)


def per_device(edge_weights, seeds, supervoxel, coarse_blocks):
    n_slab = lax.axis_size("slab")
    n_row = lax.axis_size("row")
    group = min(16, n_slab)
    sections = n_slab // group
    slab_pos = lax.axis_index("slab")
    row_pos = lax.axis_index("row")
    stacked = jnp.concatenate([edge_weights, seeds[None]], axis=0)
    lower_plane = shifted(edge_weights[0, -1:], "slab", 1)
    lower_row = shifted(edge_weights[1, :, -1:], "row", 1)
    framed = jnp.pad(stacked, ((0, 0), (1, 1), (1, 1), (0, 0)))
    framed = framed.at[0, :1, 1:-1].set(lower_plane)
    framed = framed.at[1, 1:-1, :1].set(lower_row)
    width = (framed.shape[1] - CZ) // 2
    weights = framed[:3].astype(jnp.float32) * weight_unit
    plane_ids = slab_pos * CZ - width + jnp.arange(CZ + 2 * width, dtype=jnp.int32)
    line_ids = row_pos * CY - width + jnp.arange(CY + 2 * width, dtype=jnp.int32)
    keep_z = (plane_ids != CZ * n_slab - 1).astype(jnp.float32)[:, None, None]
    keep_y = (line_ids != CY * n_row - 1).astype(jnp.float32)[None, :, None]
    keep_x = (jnp.arange(NX) < NX - 1).astype(jnp.float32)[None, None, :]
    w_z = weights[0] * keep_z
    w_y = weights[1] * keep_y
    w_x = weights[2] * keep_x
    seed_inner = crop(framed[3], 1)
    inner_x = crop(w_x, 1)
    diag = (
        prior_mass
        + seed_weight * (seed_inner >= 0).astype(jnp.float32)
        + crop(w_z, 1)
        + crop(w_y, 1)
        + inner_x
        + w_z[:-2, 1:-1]
        + w_y[1:-1, :-2]
        + lower_x(inner_x)
    )
    label_ids = jnp.arange(LABELS, dtype=jnp.int32)
    source = seed_weight * (seed_inner[None] == label_ids[:, None, None, None]).astype(jnp.float32)

    def residual_on(frame, rim):
        margin = width - rim - 1
        face_z = crop(w_z, margin)
        face_y = crop(w_y, margin)
        face_x = crop(w_x, margin)[1:-1, 1:-1]
        centre = frame[:, 1:-1, 1:-1]
        near = face_z[1:-1, 1:-1] * frame[:, 2:, 1:-1] + face_z[:-2, 1:-1] * frame[:, :-2, 1:-1]
        near = (
            near + face_y[1:-1, 1:-1] * frame[:, 1:-1, 2:] + face_y[1:-1, :-2] * frame[:, 1:-1, :-2]
        )
        near = near + face_x * upper_x(centre) + lower_x(face_x) * lower_x(centre)
        local_diag = crop(diag, width - 1 - rim)
        local_source = crop(source, width - 1 - rim)
        return (local_source - (local_diag * centre - near), local_diag, centre)

    def sweep(field):
        change, local_diag, centre = residual_on(rim_one(field), 0)
        return centre + smooth_step * change / local_diag

    block_row = coarse_blocks[0]
    turn = slab_pos // sections
    section_id = slab_pos % sections
    own_block = lax.dynamic_slice_in_dim(block_row, turn * CC, CC, 1)
    coarse_diag = jnp.diagonal(own_block)
    cells = CZ * CY * NX
    span = math.gcd(cells, 2048)
    flat_ids = supervoxel.reshape(cells)
    coarse_ids = jnp.arange(CC, dtype=jnp.int32)
    field = jnp.zeros((LABELS, CZ, CY, NX), jnp.float32)
    for cycle in range(CYCLES):
        field = sweep(sweep(field))
        residual, unused_diag, unused_centre = residual_on(rim_one(field), 0)
        flat_rows = residual.reshape(LABELS, cells)

        def collect_block(index, total):
            piece = lax.dynamic_slice_in_dim(flat_rows, index * span, span, 1)
            piece_ids = lax.dynamic_slice_in_dim(flat_ids, index * span, span, 0)
            onehot = (piece_ids[:, None] == coarse_ids[None, :]).astype(jnp.float32)
            return total + jnp.dot(
                piece, onehot, precision=lax.Precision.HIGHEST, preferred_element_type=jnp.float32
            )

        coarse_rhs = lax.fori_loop(
            0, cells // span, collect_block, jnp.zeros((LABELS, CC), jnp.float32)
        )
        first = coarse_step * coarse_rhs / coarse_diag
        gathered = lax.all_gather(first, "slab", axis=1, tiled=True)
        arranged = gathered.reshape(LABELS, group, sections, CC)
        section = lax.dynamic_slice_in_dim(arranged, section_id, 1, 2).reshape(LABELS, group * CC)
        second = (
            first
            + coarse_step
            * (
                coarse_rhs
                - lax.dot_general(
                    section,
                    block_row,
                    (((1,), (1,)), ((), ())),
                    precision=lax.Precision.HIGHEST,
                    preferred_element_type=jnp.float32,
                )
            )
            / coarse_diag
        )
        correction = jnp.take(second, flat_ids, axis=1).reshape(LABELS, CZ, CY, NX)
        field = sweep(field + correction)
    return field


def solution(mesh):
    in_specs = (
        P(None, "slab", "row", None),
        P("slab", "row", None),
        P("slab", "row", None),
        P("row", "slab", None),
    )
    out_specs = P(None, "slab", "row", None)
    return jax.shard_map(
        per_device, mesh=mesh, in_specs=in_specs, out_specs=out_specs, check_vma=False
    )
```

profile of v0, /device:TPU:6, one launch (start us, length us, event | category | flops | bytes accessed | tf_op | source)
XLA Modules:
  0.0 296.9 jit_solution(196694166765577341)
XLA Ops:
  0.0 2.6 collective-permute-start.2
  2.6 4.3 %collective-permute-start.3 = (f32[8,1,8,512]{3,2,1,0:T(8,128)S(1)}, f32[8,1,8,512]{3,2,1,0:T(8,128)S(1)}, u32[]{:S(2)}, u32[]{:S(2)}) collective-permute-start(f32[8,1,8,512]{3,2,1,0:T(8,128)S(1)} %broadcast.145), channel_id=1, source_target_pairs={{0,4},{4,8},{8,12},{12,16},{16,20},{20,24},{24,28},{1,5},{5,9},{9,... | collective-permute-start | bytes 393224 | tf_op jit(solution)/shard_map/ppermute | solution.py:28
  7.6 2.5 collective-permute-start
  16.7 3.6 %collective-permute-start.4 = (f32[8,4,1,512]{3,2,1,0:T(1,128)S(1)}, f32[8,4,1,512]{3,2,1,0:T(1,128)S(1)}, u32[]{:S(2)}, u32[]{:S(2)}) collective-permute-start(f32[8,4,1,512]{3,2,1,0:T(1,128)S(1)} %get-tuple-element.286), channel_id=1, source_target_pairs={{1,0},{2,1},{3,2},{5,4},{6,5},{7,6},{9,8},{10,9},{11,10},{13,12},{... | collective-permute-start | bytes 196616 | tf_op jit(solution)/shard_map/ppermute | solution.py:30
  22.4 3.6 %collective-permute-done.5 = f32[8,4,1,512]{3,2,1,0:T(1,128)S(1)} collective-permute-done((f32[8,4,1,512]{3,2,1,0:T(1,128)S(1)}, f32[8,4,1,512]{3,2,1,0:T(1,128)S(1)}, u32[]{:S(2)}, u32[]{:S(2)}) %collective-permute-start.5) | collective-permute-done | bytes 65568 | tf_op jit(solution)/shard_map/ppermute | solution.py:28
  26.2 3.3 %collective-permute-start.6 = (f32[8,1,8,512]{3,2,1,0:T(8,128)S(1)}, f32[8,1,8,512]{3,2,1,0:T(8,128)S(1)}, u32[]{:S(2)}, u32[]{:S(2)}) collective-permute-start(f32[8,1,8,512]{3,2,1,0:T(8,128)S(1)} %get-tuple-element.318), channel_id=1, source_target_pairs={{4,0},{8,4},{12,8},{16,12},{20,16},{24,20},{28,24},{5,1},{9,5},{13... | collective-permute-start | bytes 393224 | tf_op jit(solution)/shard_map/ppermute | solution.py:30
  29.5 3.5 %collective-permute-start.7 = (f32[8,1,8,512]{3,2,1,0:T(8,128)S(1)}, f32[8,1,8,512]{3,2,1,0:T(8,128)S(1)}, u32[]{:S(2)}, u32[]{:S(2)}) collective-permute-start(f32[8,1,8,512]{3,2,1,0:T(8,128)S(1)} %get-tuple-element.317), channel_id=1, source_target_pairs={{0,4},{4,8},{8,12},{12,16},{16,20},{20,24},{24,28},{1,5},{5,9},{9,... | collective-permute-start | bytes 393224 | tf_op jit(solution)/shard_map/ppermute | solution.py:28
  41.0 3.0 %collective-permute-done.9 = f32[8,4,1,512]{3,2,1,0:T(1,128)S(1)} collective-permute-done((f32[8,4,1,512]{3,2,1,0:T(1,128)S(1)}, f32[8,4,1,512]{3,2,1,0:T(1,128)S(1)}, u32[]{:S(2)}, u32[]{:S(2)}) %collective-permute-start.9) | collective-permute-done | bytes 65568 | tf_op jit(solution)/shard_map/ppermute | solution.py:28
  46.2 4.8 %collective-permute-start.11 = (f32[8,1,8,512]{3,2,1,0:T(8,128)S(1)}, f32[8,1,8,512]{3,2,1,0:T(8,128)S(1)}, u32[]{:S(2)}, u32[]{:S(2)}) collective-permute-start(f32[8,1,8,512]{3,2,1,0:T(8,128)S(1)} %get-tuple-element.313), channel_id=1, source_target_pairs={{0,4},{4,8},{8,12},{12,16},{16,20},{20,24},{24,28},{1,5},{5,9},{9,... | collective-permute-start | bytes 393224 | tf_op jit(solution)/shard_map/ppermute | solution.py:28
  58.1 3.0 %collective-permute-done.13 = f32[8,4,1,512]{3,2,1,0:T(1,128)S(1)} collective-permute-done((f32[8,4,1,512]{3,2,1,0:T(1,128)S(1)}, f32[8,4,1,512]{3,2,1,0:T(1,128)S(1)}, u32[]{:S(2)}, u32[]{:S(2)}) %collective-permute-start.13) | collective-permute-done | bytes 65568 | tf_op jit(solution)/shard_map/ppermute | solution.py:28
  61.6 2.5 while.30
  64.1 31.9 %all_gather.6 = f32[8,1024]{1,0:T(8,128)S(1)} all-gather(f32[8,128]{1,0:T(8,128)S(1)} %multiply_divide_fusion.1), channel_id=1, replica_groups=mesh['slab'=8,'row'=4] {'slab'}, dimensions={1}, use_global_device_ids=true | all-gather | bytes 36864 | tf_op jit(solution)/shard_map/all_gather | solution.py:143
  96.6 27.9 %gather_fusion.1 = f32[8192,8]{1,0:T(8,128)} fusion(f32[8,128]{0,1:T(8,128)S(1)} %copy.9, s32[8192]{0:T(1024)S(1)} %fusion.122), kind=kCustom, calls=%fused_computation.clone | custom fusion | bytes 557056 | tf_op jit(solution)/shard_map/jit(_take)/gather | solution.py:161
  124.5 7.5 %broadcast_select_fusion.1 = f32[8192,8]{1,0:T(8,128)} fusion(f32[8192,8]{1,0:T(8,128)} %gather_fusion.1, pred[8192]{0:T(1024)(128)(4,1)S(1)} %compare_and_fusion), kind=kLoop, calls=%fused_computation.16 | loop fusion | flops 65536 | bytes 532480 | tf_op jit(solution)/shard_map/jit(_take)/select_n | solution.py:161
  131.9 2.8 copy.10
  134.8 3.3 %collective-permute-start.14 = (f32[8,1,8,512]{3,2,1,0:T(8,128)S(1)}, f32[8,1,8,512]{3,2,1,0:T(8,128)S(1)}, u32[]{:S(2)}, u32[]{:S(2)}) collective-permute-start(f32[8,1,8,512]{3,2,1,0:T(8,128)S(1)} %get-tuple-element.310), channel_id=1, source_target_pairs={{4,0},{8,4},{12,8},{16,12},{20,16},{24,20},{28,24},{5,1},{9,5},{13... | collective-permute-start | bytes 393224 | tf_op jit(solution)/shard_map/ppermute | solution.py:30
  138.1 3.5 %collective-permute-start.15 = (f32[8,1,8,512]{3,2,1,0:T(8,128)S(1)}, f32[8,1,8,512]{3,2,1,0:T(8,128)S(1)}, u32[]{:S(2)}, u32[]{:S(2)}) collective-permute-start(f32[8,1,8,512]{3,2,1,0:T(8,128)S(1)} %get-tuple-element.309), channel_id=1, source_target_pairs={{0,4},{4,8},{8,12},{12,16},{16,20},{20,24},{24,28},{1,5},{5,9},{9,... | collective-permute-start | bytes 393224 | tf_op jit(solution)/shard_map/ppermute | solution.py:28
  149.6 3.0 %collective-permute-done.17 = f32[8,4,1,512]{3,2,1,0:T(1,128)S(1)} collective-permute-done((f32[8,4,1,512]{3,2,1,0:T(1,128)S(1)}, f32[8,4,1,512]{3,2,1,0:T(1,128)S(1)}, u32[]{:S(2)}, u32[]{:S(2)}) %collective-permute-start.17) | collective-permute-done | bytes 65568 | tf_op jit(solution)/shard_map/ppermute | solution.py:28
  154.8 4.8 %collective-permute-start.19 = (f32[8,1,8,512]{3,2,1,0:T(8,128)S(1)}, f32[8,1,8,512]{3,2,1,0:T(8,128)S(1)}, u32[]{:S(2)}, u32[]{:S(2)}) collective-permute-start(f32[8,1,8,512]{3,2,1,0:T(8,128)S(1)} %get-tuple-element.305), channel_id=1, source_target_pairs={{0,4},{4,8},{8,12},{12,16},{16,20},{20,24},{24,28},{1,5},{5,9},{9,... | collective-permute-start | bytes 393224 | tf_op jit(solution)/shard_map/ppermute | solution.py:28
  166.7 3.0 %collective-permute-done.21 = f32[8,4,1,512]{3,2,1,0:T(1,128)S(1)} collective-permute-done((f32[8,4,1,512]{3,2,1,0:T(1,128)S(1)}, f32[8,4,1,512]{3,2,1,0:T(1,128)S(1)}, u32[]{:S(2)}, u32[]{:S(2)}) %collective-permute-start.21) | collective-permute-done | bytes 65568 | tf_op jit(solution)/shard_map/ppermute | solution.py:28
  172.0 5.3 %collective-permute-start.23 = (f32[8,1,8,512]{3,2,1,0:T(8,128)S(1)}, f32[8,1,8,512]{3,2,1,0:T(8,128)S(1)}, u32[]{:S(2)}, u32[]{:S(2)}) collective-permute-start(f32[8,1,8,512]{3,2,1,0:T(8,128)S(1)} %get-tuple-element.301), channel_id=1, source_target_pairs={{0,4},{4,8},{8,12},{12,16},{16,20},{20,24},{24,28},{1,5},{5,9},{9,... | collective-permute-start | bytes 393224 | tf_op jit(solution)/shard_map/ppermute | solution.py:28
  184.4 3.0 %collective-permute-done.25 = f32[8,4,1,512]{3,2,1,0:T(1,128)S(1)} collective-permute-done((f32[8,4,1,512]{3,2,1,0:T(1,128)S(1)}, f32[8,4,1,512]{3,2,1,0:T(1,128)S(1)}, u32[]{:S(2)}, u32[]{:S(2)}) %collective-permute-start.25) | collective-permute-done | bytes 65568 | tf_op jit(solution)/shard_map/ppermute | solution.py:28
  189.7 5.2 %collective-permute-start.27 = (f32[8,1,8,512]{3,2,1,0:T(8,128)S(1)}, f32[8,1,8,512]{3,2,1,0:T(8,128)S(1)}, u32[]{:S(2)}, u32[]{:S(2)}) collective-permute-start(f32[8,1,8,512]{3,2,1,0:T(8,128)S(1)} %get-tuple-element.297), channel_id=1, source_target_pairs={{0,4},{4,8},{8,12},{12,16},{16,20},{20,24},{24,28},{1,5},{5,9},{9,... | collective-permute-start | bytes 393224 | tf_op jit(solution)/shard_map/ppermute | solution.py:28
  202.0 3.0 %collective-permute-done.29 = f32[8,4,1,512]{3,2,1,0:T(1,128)S(1)} collective-permute-done((f32[8,4,1,512]{3,2,1,0:T(1,128)S(1)}, f32[8,4,1,512]{3,2,1,0:T(1,128)S(1)}, u32[]{:S(2)}, u32[]{:S(2)}) %collective-permute-start.29) | collective-permute-done | bytes 65568 | tf_op jit(solution)/shard_map/ppermute | solution.py:28
  205.5 2.5 while.31
  208.0 30.0 %all_gather.7 = f32[8,1024]{1,0:T(8,128)S(1)} all-gather(f32[8,128]{1,0:T(8,128)S(1)} %multiply_divide_fusion), channel_id=1, replica_groups=mesh['slab'=8,'row'=4] {'slab'}, dimensions={1}, use_global_device_ids=true | all-gather | bytes 36864 | tf_op jit(solution)/shard_map/all_gather | solution.py:143
  238.6 27.9 %gather_fusion.2 = f32[8192,8]{1,0:T(8,128)} fusion(f32[8,128]{0,1:T(8,128)S(1)} %copy.11, s32[8192]{0:T(1024)S(1)} %fusion.122), kind=kCustom, calls=%fused_computation.1.clone | custom fusion | bytes 557056 | tf_op jit(solution)/shard_map/jit(_take)/gather | solution.py:161
  266.5 7.5 %broadcast_select_fusion = f32[8192,8]{1,0:T(8,128)} fusion(f32[8192,8]{1,0:T(8,128)} %gather_fusion.2, pred[8192]{0:T(1024)(128)(4,1)S(1)} %compare_and_fusion), kind=kLoop, calls=%fused_computation.15 | loop fusion | flops 65536 | bytes 532480 | tf_op jit(solution)/shard_map/jit(_take)/select_n | solution.py:161
  273.9 2.8 copy.12
  276.8 4.6 %collective-permute-start.30 = (f32[8,1,8,512]{3,2,1,0:T(8,128)S(1)}, f32[8,1,8,512]{3,2,1,0:T(8,128)S(1)}, u32[]{:S(2)}, u32[]{:S(2)}) collective-permute-start(f32[8,1,8,512]{3,2,1,0:T(8,128)S(1)} %get-tuple-element.294), channel_id=1, source_target_pairs={{4,0},{8,4},{12,8},{16,12},{20,16},{24,20},{28,24},{5,1},{9,5},{13... | collective-permute-start | bytes 393224 | tf_op jit(solution)/shard_map/ppermute | solution.py:30
  284.6 3.7 %collective-permute-done.31 = f32[8,1,8,512]{3,2,1,0:T(8,128)S(1)} collective-permute-done((f32[8,1,8,512]{3,2,1,0:T(8,128)S(1)}, f32[8,1,8,512]{3,2,1,0:T(8,128)S(1)}, u32[]{:S(2)}, u32[]{:S(2)}) %collective-permute-start.31) | collective-permute-done | bytes 131104 | tf_op jit(solution)/shard_map/ppermute | solution.py:28
  292.9 3.0 %collective-permute-done.33 = f32[8,4,1,512]{3,2,1,0:T(1,128)S(1)} collective-permute-done((f32[8,4,1,512]{3,2,1,0:T(1,128)S(1)}, f32[8,4,1,512]{3,2,1,0:T(1,128)S(1)}, u32[]{:S(2)}, u32[]{:S(2)}) %collective-permute-start.33) | collective-permute-done | bytes 65568 | tf_op jit(solution)/shard_map/ppermute | solution.py:28
  (131 shorter events, 78.0 us)
Async XLA Ops:
  0.0 16.5 %collective-permute-start.2 = (f32[8,1,8,512]{3,2,1,0:T(8,128)S(1)}, f32[8,1,8,512]{3,2,1,0:T(8,128)S(1)}, u32[]{:S(2)}, u32[]{:S(2)}) collective-permute-start(f32[8,1,8,512]{3,2,1,0:T(8,128)S(1)} %broadcast.145), channel_id=1, source_target_pairs={{4,0},{8,4},{12,8},{16,12},{20,16},{24,20},{28,24},{5,1},{9,5},{13... | collective-permute-start | bytes 393224 | tf_op jit(solution)/shard_map/ppermute | solution.py:30
  2.6 14.0 %collective-permute-start.3 = (f32[8,1,8,512]{3,2,1,0:T(8,128)S(1)}, f32[8,1,8,512]{3,2,1,0:T(8,128)S(1)}, u32[]{:S(2)}, u32[]{:S(2)}) collective-permute-start(f32[8,1,8,512]{3,2,1,0:T(8,128)S(1)} %broadcast.145), channel_id=1, source_target_pairs={{0,4},{4,8},{8,12},{12,16},{16,20},{20,24},{24,28},{1,5},{5,9},{9,... | collective-permute-start | bytes 393224 | tf_op jit(solution)/shard_map/ppermute | solution.py:28
  7.6 8.4 %collective-permute-start = (s32[1,8,512]{2,1,0:T(8,128)S(1)}, s32[1,8,512]{2,1,0:T(8,128)S(1)}, u32[]{:S(2)}, u32[]{:S(2)}) collective-permute-start(s32[1,8,512]{2,1,0:T(8,128)S(1)} %slice_bitcast_fusion.4), channel_id=1, source_target_pairs={{0,4},{4,8},{8,12},{12,16},{16,20},{20,24},{24,28},{1,5},{5,9},{9,... | collective-permute-start | bytes 49160 | tf_op jit(solution)/shard_map/ppermute | solution.py:40
  10.9 5.3 %collective-permute-start.1 = (s32[2,1,512]{2,1,0:T(1,128)S(1)}, s32[2,1,512]{2,1,0:T(1,128)S(1)}, u32[]{:S(2)}, u32[]{:S(2)}) collective-permute-start(s32[2,1,512]{2,1,0:T(1,128)S(1)} %slice_bitcast_fusion.5), channel_id=1, source_target_pairs={{0,1},{1,2},{2,3},{4,5},{5,6},{6,7},{8,9},{9,10},{10,11},{12,13},{... | collective-permute-start | bytes 12296 | tf_op jit(solution)/shard_map/ppermute | solution.py:40
  16.7 5.7 %collective-permute-start.4 = (f32[8,4,1,512]{3,2,1,0:T(1,128)S(1)}, f32[8,4,1,512]{3,2,1,0:T(1,128)S(1)}, u32[]{:S(2)}, u32[]{:S(2)}) collective-permute-start(f32[8,4,1,512]{3,2,1,0:T(1,128)S(1)} %get-tuple-element.286), channel_id=1, source_target_pairs={{1,0},{2,1},{3,2},{5,4},{6,5},{7,6},{9,8},{10,9},{11,10},{13,12},{... | collective-permute-start | bytes 196616 | tf_op jit(solution)/shard_map/ppermute | solution.py:30
  20.3 5.6 %collective-permute-start.5 = (f32[8,4,1,512]{3,2,1,0:T(1,128)S(1)}, f32[8,4,1,512]{3,2,1,0:T(1,128)S(1)}, u32[]{:S(2)}, u32[]{:S(2)}) collective-permute-start(f32[8,4,1,512]{3,2,1,0:T(1,128)S(1)} %get-tuple-element.287), channel_id=1, source_target_pairs={{0,1},{1,2},{2,3},{4,5},{5,6},{6,7},{8,9},{9,10},{10,11},{12,13},{... | collective-permute-start | bytes 196616 | tf_op jit(solution)/shard_map/ppermute | solution.py:28
  26.2 7.9 %collective-permute-start.6 = (f32[8,1,8,512]{3,2,1,0:T(8,128)S(1)}, f32[8,1,8,512]{3,2,1,0:T(8,128)S(1)}, u32[]{:S(2)}, u32[]{:S(2)}) collective-permute-start(f32[8,1,8,512]{3,2,1,0:T(8,128)S(1)} %get-tuple-element.318), channel_id=1, source_target_pairs={{4,0},{8,4},{12,8},{16,12},{20,16},{24,20},{28,24},{5,1},{9,5},{13... | collective-permute-start | bytes 393224 | tf_op jit(solution)/shard_map/ppermute | solution.py:30
  29.5 6.9 %collective-permute-start.7 = (f32[8,1,8,512]{3,2,1,0:T(8,128)S(1)}, f32[8,1,8,512]{3,2,1,0:T(8,128)S(1)}, u32[]{:S(2)}, u32[]{:S(2)}) collective-permute-start(f32[8,1,8,512]{3,2,1,0:T(8,128)S(1)} %get-tuple-element.317), channel_id=1, source_target_pairs={{0,4},{4,8},{8,12},{12,16},{16,20},{20,24},{24,28},{1,5},{5,9},{9,... | collective-permute-start | bytes 393224 | tf_op jit(solution)/shard_map/ppermute | solution.py:28
  36.5 4.5 %collective-permute-start.8 = (f32[8,4,1,512]{3,2,1,0:T(1,128)S(1)}, f32[8,4,1,512]{3,2,1,0:T(1,128)S(1)}, u32[]{:S(2)}, u32[]{:S(2)}) collective-permute-start(f32[8,4,1,512]{3,2,1,0:T(1,128)S(1)} %get-tuple-element.284), channel_id=1, source_target_pairs={{1,0},{2,1},{3,2},{5,4},{6,5},{7,6},{9,8},{10,9},{11,10},{13,12},{... | collective-permute-start | bytes 196616 | tf_op jit(solution)/shard_map/ppermute | solution.py:30
  38.4 5.6 %collective-permute-start.9 = (f32[8,4,1,512]{3,2,1,0:T(1,128)S(1)}, f32[8,4,1,512]{3,2,1,0:T(1,128)S(1)}, u32[]{:S(2)}, u32[]{:S(2)}) collective-permute-start(f32[8,4,1,512]{3,2,1,0:T(1,128)S(1)} %get-tuple-element.285), channel_id=1, source_target_pairs={{0,1},{1,2},{2,3},{4,5},{5,6},{6,7},{8,9},{9,10},{10,11},{12,13},{... | collective-permute-start | bytes 196616 | tf_op jit(solution)/shard_map/ppermute | solution.py:28
  44.3 7.8 %collective-permute-start.10 = (f32[8,1,8,512]{3,2,1,0:T(8,128)S(1)}, f32[8,1,8,512]{3,2,1,0:T(8,128)S(1)}, u32[]{:S(2)}, u32[]{:S(2)}) collective-permute-start(f32[8,1,8,512]{3,2,1,0:T(8,128)S(1)} %get-tuple-element.314), channel_id=1, source_target_pairs={{4,0},{8,4},{12,8},{16,12},{20,16},{24,20},{28,24},{5,1},{9,5},{13... | collective-permute-start | bytes 393224 | tf_op jit(solution)/shard_map/ppermute | solution.py:30
  46.2 7.3 %collective-permute-start.11 = (f32[8,1,8,512]{3,2,1,0:T(8,128)S(1)}, f32[8,1,8,512]{3,2,1,0:T(8,128)S(1)}, u32[]{:S(2)}, u32[]{:S(2)}) collective-permute-start(f32[8,1,8,512]{3,2,1,0:T(8,128)S(1)} %get-tuple-element.313), channel_id=1, source_target_pairs={{0,4},{4,8},{8,12},{12,16},{16,20},{20,24},{24,28},{1,5},{5,9},{9,... | collective-permute-start | bytes 393224 | tf_op jit(solution)/shard_map/ppermute | solution.py:28
  53.6 4.5 %collective-permute-start.12 = (f32[8,4,1,512]{3,2,1,0:T(1,128)S(1)}, f32[8,4,1,512]{3,2,1,0:T(1,128)S(1)}, u32[]{:S(2)}, u32[]{:S(2)}) collective-permute-start(f32[8,4,1,512]{3,2,1,0:T(1,128)S(1)} %get-tuple-element.282), channel_id=1, source_target_pairs={{1,0},{2,1},{3,2},{5,4},{6,5},{7,6},{9,8},{10,9},{11,10},{13,12},{... | collective-permute-start | bytes 196616 | tf_op jit(solution)/shard_map/ppermute | solution.py:30
  55.6 5.6 %collective-permute-start.13 = (f32[8,4,1,512]{3,2,1,0:T(1,128)S(1)}, f32[8,4,1,512]{3,2,1,0:T(1,128)S(1)}, u32[]{:S(2)}, u32[]{:S(2)}) collective-permute-start(f32[8,4,1,512]{3,2,1,0:T(1,128)S(1)} %get-tuple-element.283), channel_id=1, source_target_pairs={{0,1},{1,2},{2,3},{4,5},{5,6},{6,7},{8,9},{9,10},{10,11},{12,13},{... | collective-permute-start | bytes 196616 | tf_op jit(solution)/shard_map/ppermute | solution.py:28
  134.8 7.8 %collective-permute-start.14 = (f32[8,1,8,512]{3,2,1,0:T(8,128)S(1)}, f32[8,1,8,512]{3,2,1,0:T(8,128)S(1)}, u32[]{:S(2)}, u32[]{:S(2)}) collective-permute-start(f32[8,1,8,512]{3,2,1,0:T(8,128)S(1)} %get-tuple-element.310), channel_id=1, source_target_pairs={{4,0},{8,4},{12,8},{16,12},{20,16},{24,20},{28,24},{5,1},{9,5},{13... | collective-permute-start | bytes 393224 | tf_op jit(solution)/shard_map/ppermute | solution.py:30
  138.1 6.9 %collective-permute-start.15 = (f32[8,1,8,512]{3,2,1,0:T(8,128)S(1)}, f32[8,1,8,512]{3,2,1,0:T(8,128)S(1)}, u32[]{:S(2)}, u32[]{:S(2)}) collective-permute-start(f32[8,1,8,512]{3,2,1,0:T(8,128)S(1)} %get-tuple-element.309), channel_id=1, source_target_pairs={{0,4},{4,8},{8,12},{12,16},{16,20},{20,24},{24,28},{1,5},{5,9},{9,... | collective-permute-start | bytes 393224 | tf_op jit(solution)/shard_map/ppermute | solution.py:28
  145.1 4.5 %collective-permute-start.16 = (f32[8,4,1,512]{3,2,1,0:T(1,128)S(1)}, f32[8,4,1,512]{3,2,1,0:T(1,128)S(1)}, u32[]{:S(2)}, u32[]{:S(2)}) collective-permute-start(f32[8,4,1,512]{3,2,1,0:T(1,128)S(1)} %get-tuple-element.280), channel_id=1, source_target_pairs={{1,0},{2,1},{3,2},{5,4},{6,5},{7,6},{9,8},{10,9},{11,10},{13,12},{... | collective-permute-start | bytes 196616 | tf_op jit(solution)/shard_map/ppermute | solution.py:30
  147.0 5.6 %collective-permute-start.17 = (f32[8,4,1,512]{3,2,1,0:T(1,128)S(1)}, f32[8,4,1,512]{3,2,1,0:T(1,128)S(1)}, u32[]{:S(2)}, u32[]{:S(2)}) collective-permute-start(f32[8,4,1,512]{3,2,1,0:T(1,128)S(1)} %get-tuple-element.281), channel_id=1, source_target_pairs={{0,1},{1,2},{2,3},{4,5},{5,6},{6,7},{8,9},{9,10},{10,11},{12,13},{... | collective-permute-start | bytes 196616 | tf_op jit(solution)/shard_map/ppermute | solution.py:28
  152.9 7.8 %collective-permute-start.18 = (f32[8,1,8,512]{3,2,1,0:T(8,128)S(1)}, f32[8,1,8,512]{3,2,1,0:T(8,128)S(1)}, u32[]{:S(2)}, u32[]{:S(2)}) collective-permute-start(f32[8,1,8,512]{3,2,1,0:T(8,128)S(1)} %get-tuple-element.306), channel_id=1, source_target_pairs={{4,0},{8,4},{12,8},{16,12},{20,16},{24,20},{28,24},{5,1},{9,5},{13... | collective-permute-start | bytes 393224 | tf_op jit(solution)/shard_map/ppermute | solution.py:30
  154.8 7.3 %collective-permute-start.19 = (f32[8,1,8,512]{3,2,1,0:T(8,128)S(1)}, f32[8,1,8,512]{3,2,1,0:T(8,128)S(1)}, u32[]{:S(2)}, u32[]{:S(2)}) collective-permute-start(f32[8,1,8,512]{3,2,1,0:T(8,128)S(1)} %get-tuple-element.305), channel_id=1, source_target_pairs={{0,4},{4,8},{8,12},{12,16},{16,20},{20,24},{24,28},{1,5},{5,9},{9,... | collective-permute-start | bytes 393224 | tf_op jit(solution)/shard_map/ppermute | solution.py:28
  164.2 5.6 %collective-permute-start.21 = (f32[8,4,1,512]{3,2,1,0:T(1,128)S(1)}, f32[8,4,1,512]{3,2,1,0:T(1,128)S(1)}, u32[]{:S(2)}, u32[]{:S(2)}) collective-permute-start(f32[8,4,1,512]{3,2,1,0:T(1,128)S(1)} %get-tuple-element.279), channel_id=1, source_target_pairs={{0,1},{1,2},{2,3},{4,5},{5,6},{6,7},{8,9},{9,10},{10,11},{12,13},{... | collective-permute-start | bytes 196616 | tf_op jit(solution)/shard_map/ppermute | solution.py:28
  170.1 8.3 %collective-permute-start.22 = (f32[8,1,8,512]{3,2,1,0:T(8,128)S(1)}, f32[8,1,8,512]{3,2,1,0:T(8,128)S(1)}, u32[]{:S(2)}, u32[]{:S(2)}) collective-permute-start(f32[8,1,8,512]{3,2,1,0:T(8,128)S(1)} %get-tuple-element.302), channel_id=1, source_target_pairs={{4,0},{8,4},{12,8},{16,12},{20,16},{24,20},{28,24},{5,1},{9,5},{13... | collective-permute-start | bytes 393224 | tf_op jit(solution)/shard_map/ppermute | solution.py:30
  172.0 7.8 %collective-permute-start.23 = (f32[8,1,8,512]{3,2,1,0:T(8,128)S(1)}, f32[8,1,8,512]{3,2,1,0:T(8,128)S(1)}, u32[]{:S(2)}, u32[]{:S(2)}) collective-permute-start(f32[8,1,8,512]{3,2,1,0:T(8,128)S(1)} %get-tuple-element.301), channel_id=1, source_target_pairs={{0,4},{4,8},{8,12},{12,16},{16,20},{20,24},{24,28},{1,5},{5,9},{9,... | collective-permute-start | bytes 393224 | tf_op jit(solution)/shard_map/ppermute | solution.py:28
  179.9 4.5 %collective-permute-start.24 = (f32[8,4,1,512]{3,2,1,0:T(1,128)S(1)}, f32[8,4,1,512]{3,2,1,0:T(1,128)S(1)}, u32[]{:S(2)}, u32[]{:S(2)}) collective-permute-start(f32[8,4,1,512]{3,2,1,0:T(1,128)S(1)} %get-tuple-element.276), channel_id=1, source_target_pairs={{1,0},{2,1},{3,2},{5,4},{6,5},{7,6},{9,8},{10,9},{11,10},{13,12},{... | collective-permute-start | bytes 196616 | tf_op jit(solution)/shard_map/ppermute | solution.py:30
  181.9 5.6 %collective-permute-start.25 = (f32[8,4,1,512]{3,2,1,0:T(1,128)S(1)}, f32[8,4,1,512]{3,2,1,0:T(1,128)S(1)}, u32[]{:S(2)}, u32[]{:S(2)}) collective-permute-start(f32[8,4,1,512]{3,2,1,0:T(1,128)S(1)} %get-tuple-element.277), channel_id=1, source_target_pairs={{0,1},{1,2},{2,3},{4,5},{5,6},{6,7},{8,9},{9,10},{10,11},{12,13},{... | collective-permute-start | bytes 196616 | tf_op jit(solution)/shard_map/ppermute | solution.py:28
  187.8 8.2 %collective-permute-start.26 = (f32[8,1,8,512]{3,2,1,0:T(8,128)S(1)}, f32[8,1,8,512]{3,2,1,0:T(8,128)S(1)}, u32[]{:S(2)}, u32[]{:S(2)}) collective-permute-start(f32[8,1,8,512]{3,2,1,0:T(8,128)S(1)} %get-tuple-element.298), channel_id=1, source_target_pairs={{4,0},{8,4},{12,8},{16,12},{20,16},{24,20},{28,24},{5,1},{9,5},{13... | collective-permute-start | bytes 393224 | tf_op jit(solution)/shard_map/ppermute | solution.py:30
  189.7 7.8 %collective-permute-start.27 = (f32[8,1,8,512]{3,2,1,0:T(8,128)S(1)}, f32[8,1,8,512]{3,2,1,0:T(8,128)S(1)}, u32[]{:S(2)}, u32[]{:S(2)}) collective-permute-start(f32[8,1,8,512]{3,2,1,0:T(8,128)S(1)} %get-tuple-element.297), channel_id=1, source_target_pairs={{0,4},{4,8},{8,12},{12,16},{16,20},{20,24},{24,28},{1,5},{5,9},{9,... | collective-permute-start | bytes 393224 | tf_op jit(solution)/shard_map/ppermute | solution.py:28
  197.5 4.5 %collective-permute-start.28 = (f32[8,4,1,512]{3,2,1,0:T(1,128)S(1)}, f32[8,4,1,512]{3,2,1,0:T(1,128)S(1)}, u32[]{:S(2)}, u32[]{:S(2)}) collective-permute-start(f32[8,4,1,512]{3,2,1,0:T(1,128)S(1)} %get-tuple-element.274), channel_id=1, source_target_pairs={{1,0},{2,1},{3,2},{5,4},{6,5},{7,6},{9,8},{10,9},{11,10},{13,12},{... | collective-permute-start | bytes 196616 | tf_op jit(solution)/shard_map/ppermute | solution.py:30
  199.5 5.6 %collective-permute-start.29 = (f32[8,4,1,512]{3,2,1,0:T(1,128)S(1)}, f32[8,4,1,512]{3,2,1,0:T(1,128)S(1)}, u32[]{:S(2)}, u32[]{:S(2)}) collective-permute-start(f32[8,4,1,512]{3,2,1,0:T(1,128)S(1)} %get-tuple-element.275), channel_id=1, source_target_pairs={{0,1},{1,2},{2,3},{4,5},{5,6},{6,7},{8,9},{9,10},{10,11},{12,13},{... | collective-permute-start | bytes 196616 | tf_op jit(solution)/shard_map/ppermute | solution.py:28
  276.8 7.8 %collective-permute-start.30 = (f32[8,1,8,512]{3,2,1,0:T(8,128)S(1)}, f32[8,1,8,512]{3,2,1,0:T(8,128)S(1)}, u32[]{:S(2)}, u32[]{:S(2)}) collective-permute-start(f32[8,1,8,512]{3,2,1,0:T(8,128)S(1)} %get-tuple-element.294), channel_id=1, source_target_pairs={{4,0},{8,4},{12,8},{16,12},{20,16},{24,20},{28,24},{5,1},{9,5},{13... | collective-permute-start | bytes 393224 | tf_op jit(solution)/shard_map/ppermute | solution.py:30
  281.4 6.9 %collective-permute-start.31 = (f32[8,1,8,512]{3,2,1,0:T(8,128)S(1)}, f32[8,1,8,512]{3,2,1,0:T(8,128)S(1)}, u32[]{:S(2)}, u32[]{:S(2)}) collective-permute-start(f32[8,1,8,512]{3,2,1,0:T(8,128)S(1)} %get-tuple-element.293), channel_id=1, source_target_pairs={{0,4},{4,8},{8,12},{12,16},{16,20},{20,24},{24,28},{1,5},{5,9},{9,... | collective-permute-start | bytes 393224 | tf_op jit(solution)/shard_map/ppermute | solution.py:28
  290.3 5.6 %collective-permute-start.33 = (f32[8,4,1,512]{3,2,1,0:T(1,128)S(1)}, f32[8,4,1,512]{3,2,1,0:T(1,128)S(1)}, u32[]{:S(2)}, u32[]{:S(2)}) collective-permute-start(f32[8,4,1,512]{3,2,1,0:T(1,128)S(1)} %get-tuple-element.273), channel_id=1, source_target_pairs={{0,1},{1,2},{2,3},{4,5},{5,6},{6,7},{8,9},{9,10},{10,11},{12,13},{... | collective-permute-start | bytes 196616 | tf_op jit(solution)/shard_map/ppermute | solution.py:28
  (3 other events, 22.8 us)
where the time goes:
time: 298 us; the launch traced here: 297 us
  starting transfers between devices  95.1 us (32%)
  local copies, waits for them, and re-layouts  66.9 us (22%)
  blocking collectives  61.9 us (21%)
  waiting for transfers between devices  46.4 us (16%)
  other arithmetic  19.8 us (7%)
  matrix products  5.65 us (2%)
    all_gather x2, blocking collectives, per_device(): gathered = lax.all_gather(first, 'slab', axis=1, tiled=True)  61.9 us
    gather x2, local copies, waits for them, and re-layouts, per_device(): correction = jnp.take(second, flat_ids, axis=1).reshape(LABELS, CZ, CY, NX)  55.7 us
    ppermute x16, starting transfers between devices, padded(): lax.ppermute(tail, axis, [(i, (i + 1) % count) for i in range(ends)])  52.2 us
    ppermute x16, waiting for transfers between devices, padded(): lax.ppermute(tail, axis, [(i, (i + 1) % count) for i in range(ends)])  39 us
    ppermute x16, starting transfers between devices, padded(): lax.ppermute(head, axis, [((i + 1) % count, i) for i in range(ends)])  38.5 us
    select_n x2, other arithmetic, per_device(): correction = jnp.take(second, flat_ids, axis=1).reshape(LABELS, CZ, CY, NX)  14.9 us
    ppermute x16, waiting for transfers between devices, padded(): lax.ppermute(head, axis, [((i + 1) % count, i) for i in range(ends)])  7.38 us
  transfers between devices with their start and end apart: 34, of which 22 were waited for; matrix products, arithmetic and copies ran while one was open for 2% of the time, Pallas kernels for 0%

commit v1 on v0

--- a/solution.py
+++ b/solution.py
@@ -15,6 +15,24 @@
 smooth_step = 0.8
 coarse_step = 0.7
 weight_unit = 0.125
+
+
+def laid_out(parts, dim):
+    parts = jnp.moveaxis(parts, 0, dim)
+    shape = parts.shape
+    return parts.reshape(*shape[:dim], shape[dim] * shape[dim + 1], *shape[dim + 2 :])
+
+
+def collected_by_bits(x, axis):
+    size = lax.axis_size(axis)
+    parts = x[None]
+    for level in range(size.bit_length() - 1):
+        distance = 1 << level
+        received = lax.ppermute(parts, axis, [(i, i ^ distance) for i in range(size)])
+        both = jnp.stack([parts, received])
+        upper = lax.axis_index(axis) >> level & 1
+        parts = jnp.where(upper == 0, both, both[::-1]).reshape(-1, *x.shape)
+    return parts
 
 
 def padded(cells, sides, width):
@@ -140,7 +158,7 @@
             0, cells // span, collect_block, jnp.zeros((LABELS, CC), jnp.float32)
         )
         first = coarse_step * coarse_rhs / coarse_diag
-        gathered = lax.all_gather(first, "slab", axis=1, tiled=True)
+        gathered = laid_out(collected_by_bits(first, "slab"), 1)
         arranged = gathered.reshape(LABELS, group, sections, CC)
         section = lax.dynamic_slice_in_dim(arranged, section_id, 1, 2).reshape(LABELS, group * CC)
         second = (

time: 298 us -> 260 us (0.87)
  blocking collectives: 61.9 us -> 0 us
  waiting for transfers between devices: 46.4 us -> 58.7 us
  starting transfers between devices: 95.1 us -> 106 us
    all_gather x2 -> x0, blocking collectives: 61.9 us -> none  [per_device(): gathered = lax.all_gather(first, 'slab', axis=1, tiled=True)]
    ppermute x0 -> x6, waiting for transfers between devices: none -> 13.8 us  [collected_by_bits(): lax.ppermute(parts, axis, [(i, i ^ distance) for i in range(size)])]
    ppermute x0 -> x6, starting transfers between devices: none -> 12.2 us  [collected_by_bits(): lax.ppermute(parts, axis, [(i, i ^ distance) for i in range(size)])]
    ppermute x16, starting transfers between devices: 38.5 us -> 35.5 us  [padded(): lax.ppermute(head, axis, [((i + 1) % count, i) for i in range(ends)])]
  transfers between devices with their start and end apart: 34 -> 40, of which waited for: 22 -> 28; matrix products, arithmetic and copies ran while one was open for 2% -> 2% of each run, Pallas kernels for 0% -> 0%
where the time goes in v1:
time: 260 us; the launch traced here: 257 us
  starting transfers between devices  106 us (41%)
  local copies, waits for them, and re-layouts  65.8 us (25%)
  waiting for transfers between devices  58.7 us (23%)
  other arithmetic  19.9 us (8%)
  matrix products  5.66 us (2%)
    gather x2, local copies, waits for them, and re-layouts, per_device(): correction = jnp.take(second, flat_ids, axis=1).reshape(LABELS, CZ, CY, NX)  55.4 us
    ppermute x16, starting transfers between devices, padded(): lax.ppermute(tail, axis, [(i, (i + 1) % count) for i in range(ends)])  54.1 us
    ppermute x16, waiting for transfers between devices, padded(): lax.ppermute(tail, axis, [(i, (i + 1) % count) for i in range(ends)])  36.7 us
    ppermute x16, starting transfers between devices, padded(): lax.ppermute(head, axis, [((i + 1) % count, i) for i in range(ends)])  35.5 us
    select_n x2, other arithmetic, per_device(): correction = jnp.take(second, flat_ids, axis=1).reshape(LABELS, CZ, CY, NX)  14.9 us
    ppermute x6, waiting for transfers between devices, collected_by_bits(): lax.ppermute(parts, axis, [(i, i ^ distance) for i in range(size)])  13.8 us
    ppermute x6, starting transfers between devices, collected_by_bits(): lax.ppermute(parts, axis, [(i, i ^ distance) for i in range(size)])  12.2 us
    ppermute x16, waiting for transfers between devices, padded(): lax.ppermute(head, axis, [((i + 1) % count, i) for i in range(ends)])  6.38 us
  transfers between devices with their start and end apart: 40, of which 28 were waited for; matrix products, arithmetic and copies ran while one was open for 2% of the time, Pallas kernels for 0%

profile of v1, /device:TPU:6, one launch (start us, length us, event | category | flops | bytes accessed | tf_op | source)
XLA Modules:
  0.0 257.4 jit_solution(11656950284326380178)
XLA Ops:
  0.0 2.6 %collective-permute-start.2 = (f32[8,1,8,512]{3,2,1,0:T(8,128)S(1)}, f32[8,1,8,512]{3,2,1,0:T(8,128)S(1)}, u32[]{:S(2)}, u32[]{:S(2)}) collective-permute-start(f32[8,1,8,512]{3,2,1,0:T(8,128)S(1)} %broadcast.145), channel_id=1, source_target_pairs={{4,0},{8,4},{12,8},{16,12},{20,16},{24,20},{28,24},{5,1},{9,5},{13... | collective-permute-start | bytes 393224 | tf_op jit(solution)/shard_map/ppermute | solution.py:48
  2.6 4.3 %collective-permute-start.3 = (f32[8,1,8,512]{3,2,1,0:T(8,128)S(1)}, f32[8,1,8,512]{3,2,1,0:T(8,128)S(1)}, u32[]{:S(2)}, u32[]{:S(2)}) collective-permute-start(f32[8,1,8,512]{3,2,1,0:T(8,128)S(1)} %broadcast.145), channel_id=1, source_target_pairs={{0,4},{4,8},{8,12},{12,16},{16,20},{20,24},{24,28},{1,5},{5,9},{9,... | collective-permute-start | bytes 393224 | tf_op jit(solution)/shard_map/ppermute | solution.py:46
  20.8 3.1 %collective-permute-done.5 = f32[8,4,1,512]{3,2,1,0:T(1,128)S(1)} collective-permute-done((f32[8,4,1,512]{3,2,1,0:T(1,128)S(1)}, f32[8,4,1,512]{3,2,1,0:T(1,128)S(1)}, u32[]{:S(2)}, u32[]{:S(2)}) %collective-permute-start.5) | collective-permute-done | bytes 65568 | tf_op jit(solution)/shard_map/ppermute | solution.py:46
  24.2 3.3 %collective-permute-start.6 = (f32[8,1,8,512]{3,2,1,0:T(8,128)S(1)}, f32[8,1,8,512]{3,2,1,0:T(8,128)S(1)}, u32[]{:S(2)}, u32[]{:S(2)}) collective-permute-start(f32[8,1,8,512]{3,2,1,0:T(8,128)S(1)} %get-tuple-element.318), channel_id=1, source_target_pairs={{4,0},{8,4},{12,8},{16,12},{20,16},{24,20},{28,24},{5,1},{9,5},{13... | collective-permute-start | bytes 393224 | tf_op jit(solution)/shard_map/ppermute | solution.py:48
  27.4 3.5 %collective-permute-start.7 = (f32[8,1,8,512]{3,2,1,0:T(8,128)S(1)}, f32[8,1,8,512]{3,2,1,0:T(8,128)S(1)}, u32[]{:S(2)}, u32[]{:S(2)}) collective-permute-start(f32[8,1,8,512]{3,2,1,0:T(8,128)S(1)} %get-tuple-element.317), channel_id=1, source_target_pairs={{0,4},{4,8},{8,12},{12,16},{16,20},{20,24},{24,28},{1,5},{5,9},{9,... | collective-permute-start | bytes 393224 | tf_op jit(solution)/shard_map/ppermute | solution.py:46
  38.9 3.0 %collective-permute-done.9 = f32[8,4,1,512]{3,2,1,0:T(1,128)S(1)} collective-permute-done((f32[8,4,1,512]{3,2,1,0:T(1,128)S(1)}, f32[8,4,1,512]{3,2,1,0:T(1,128)S(1)}, u32[]{:S(2)}, u32[]{:S(2)}) %collective-permute-start.9) | collective-permute-done | bytes 65568 | tf_op jit(solution)/shard_map/ppermute | solution.py:46
  44.1 4.8 %collective-permute-start.11 = (f32[8,1,8,512]{3,2,1,0:T(8,128)S(1)}, f32[8,1,8,512]{3,2,1,0:T(8,128)S(1)}, u32[]{:S(2)}, u32[]{:S(2)}) collective-permute-start(f32[8,1,8,512]{3,2,1,0:T(8,128)S(1)} %get-tuple-element.313), channel_id=1, source_target_pairs={{0,4},{4,8},{8,12},{12,16},{16,20},{20,24},{24,28},{1,5},{5,9},{9,... | collective-permute-start | bytes 393224 | tf_op jit(solution)/shard_map/ppermute | solution.py:46
  56.1 3.0 %collective-permute-done.13 = f32[8,4,1,512]{3,2,1,0:T(1,128)S(1)} collective-permute-done((f32[8,4,1,512]{3,2,1,0:T(1,128)S(1)}, f32[8,4,1,512]{3,2,1,0:T(1,128)S(1)}, u32[]{:S(2)}, u32[]{:S(2)}) %collective-permute-start.13) | collective-permute-done | bytes 65568 | tf_op jit(solution)/shard_map/ppermute | solution.py:46
  62.1 3.6 %collective-permute-done.14 = f32[1,8,128]{2,1,0:T(8,128)S(1)} collective-permute-done((f32[1,8,128]{2,1,0:T(8,128)S(1)}, f32[1,8,128]{2,1,0:T(8,128)S(1)}, u32[]{:S(2)}, u32[]{:S(2)}) %collective-permute-start.14) | collective-permute-done | bytes 4128 | tf_op jit(solution)/shard_map/ppermute | solution.py:31
  69.9 3.0 %collective-permute-start.16 = (f32[4,8,128]{2,1,0:T(8,128)S(1)}, f32[4,8,128]{2,1,0:T(8,128)S(1)}, u32[]{:S(2)}, u32[]{:S(2)}) collective-permute-start(f32[4,8,128]{2,1,0:T(8,128)S(1)} %bitcast.99), channel_id=1, source_target_pairs={{0,16},{4,20},{8,24},{12,28},{16,0},{20,4},{24,8},{28,12},{1,17},{... | collective-permute-start | bytes 49160 | tf_op jit(solution)/shard_map/ppermute | solution.py:31
  75.3 27.7 %gather_fusion.1 = f32[8192,8]{1,0:T(8,128)} fusion(f32[8,128]{0,1:T(8,128)S(1)} %copy.12, s32[8192]{0:T(1024)S(1)} %fusion.122), kind=kCustom, calls=%fused_computation.clone | custom fusion | bytes 557056 | tf_op jit(solution)/shard_map/jit(_take)/gather | solution.py:179
  102.9 7.4 %broadcast_select_fusion.1 = f32[8192,8]{1,0:T(8,128)} fusion(f32[8192,8]{1,0:T(8,128)} %gather_fusion.1, pred[8192]{0:T(1024)(128)(4,1)S(1)} %compare_and_fusion), kind=kLoop, calls=%fused_computation.16 | loop fusion | flops 65536 | bytes 532480 | tf_op jit(solution)/shard_map/jit(_take)/select_n | solution.py:179
  110.4 2.8 %copy.13 = f32[8,2,8,512]{3,2,1,0:T(8,128)S(1)} copy(f32[8,2,8,512]{0,3,2,1:T(8,128)} %bitcast.93) | data formatting | bytes 524288 | tf_op jit(solution)/shard_map/reshape | solution.py:179
  113.3 3.3 %collective-permute-start.17 = (f32[8,1,8,512]{3,2,1,0:T(8,128)S(1)}, f32[8,1,8,512]{3,2,1,0:T(8,128)S(1)}, u32[]{:S(2)}, u32[]{:S(2)}) collective-permute-start(f32[8,1,8,512]{3,2,1,0:T(8,128)S(1)} %get-tuple-element.310), channel_id=1, source_target_pairs={{4,0},{8,4},{12,8},{16,12},{20,16},{24,20},{28,24},{5,1},{9,5},{13... | collective-permute-start | bytes 393224 | tf_op jit(solution)/shard_map/ppermute | solution.py:48
  116.6 3.5 %collective-permute-start.18 = (f32[8,1,8,512]{3,2,1,0:T(8,128)S(1)}, f32[8,1,8,512]{3,2,1,0:T(8,128)S(1)}, u32[]{:S(2)}, u32[]{:S(2)}) collective-permute-start(f32[8,1,8,512]{3,2,1,0:T(8,128)S(1)} %get-tuple-element.309), channel_id=1, source_target_pairs={{0,4},{4,8},{8,12},{12,16},{16,20},{20,24},{24,28},{1,5},{5,9},{9,... | collective-permute-start | bytes 393224 | tf_op jit(solution)/shard_map/ppermute | solution.py:46
  128.0 3.0 %collective-permute-done.20 = f32[8,4,1,512]{3,2,1,0:T(1,128)S(1)} collective-permute-done((f32[8,4,1,512]{3,2,1,0:T(1,128)S(1)}, f32[8,4,1,512]{3,2,1,0:T(1,128)S(1)}, u32[]{:S(2)}, u32[]{:S(2)}) %collective-permute-start.20) | collective-permute-done | bytes 65568 | tf_op jit(solution)/shard_map/ppermute | solution.py:46
  133.3 4.8 %collective-permute-start.22 = (f32[8,1,8,512]{3,2,1,0:T(8,128)S(1)}, f32[8,1,8,512]{3,2,1,0:T(8,128)S(1)}, u32[]{:S(2)}, u32[]{:S(2)}) collective-permute-start(f32[8,1,8,512]{3,2,1,0:T(8,128)S(1)} %get-tuple-element.305), channel_id=1, source_target_pairs={{0,4},{4,8},{8,12},{12,16},{16,20},{20,24},{24,28},{1,5},{5,9},{9,... | collective-permute-start | bytes 393224 | tf_op jit(solution)/shard_map/ppermute | solution.py:46
  145.2 3.0 %collective-permute-done.24 = f32[8,4,1,512]{3,2,1,0:T(1,128)S(1)} collective-permute-done((f32[8,4,1,512]{3,2,1,0:T(1,128)S(1)}, f32[8,4,1,512]{3,2,1,0:T(1,128)S(1)}, u32[]{:S(2)}, u32[]{:S(2)}) %collective-permute-start.24) | collective-permute-done | bytes 65568 | tf_op jit(solution)/shard_map/ppermute | solution.py:46
  150.5 5.3 %collective-permute-start.26 = (f32[8,1,8,512]{3,2,1,0:T(8,128)S(1)}, f32[8,1,8,512]{3,2,1,0:T(8,128)S(1)}, u32[]{:S(2)}, u32[]{:S(2)}) collective-permute-start(f32[8,1,8,512]{3,2,1,0:T(8,128)S(1)} %get-tuple-element.301), channel_id=1, source_target_pairs={{0,4},{4,8},{8,12},{12,16},{16,20},{20,24},{24,28},{1,5},{5,9},{9,... | collective-permute-start | bytes 393224 | tf_op jit(solution)/shard_map/ppermute | solution.py:46
  162.9 3.0 %collective-permute-done.28 = f32[8,4,1,512]{3,2,1,0:T(1,128)S(1)} collective-permute-done((f32[8,4,1,512]{3,2,1,0:T(1,128)S(1)}, f32[8,4,1,512]{3,2,1,0:T(1,128)S(1)}, u32[]{:S(2)}, u32[]{:S(2)}) %collective-permute-start.28) | collective-permute-done | bytes 65568 | tf_op jit(solution)/shard_map/ppermute | solution.py:46
  168.1 5.2 %collective-permute-start.30 = (f32[8,1,8,512]{3,2,1,0:T(8,128)S(1)}, f32[8,1,8,512]{3,2,1,0:T(8,128)S(1)}, u32[]{:S(2)}, u32[]{:S(2)}) collective-permute-start(f32[8,1,8,512]{3,2,1,0:T(8,128)S(1)} %get-tuple-element.297), channel_id=1, source_target_pairs={{0,4},{4,8},{8,12},{12,16},{16,20},{20,24},{24,28},{1,5},{5,9},{9,... | collective-permute-start | bytes 393224 | tf_op jit(solution)/shard_map/ppermute | solution.py:46
  177.9 2.6 %collective-permute-start.32 = (f32[8,4,1,512]{3,2,1,0:T(1,128)S(1)}, f32[8,4,1,512]{3,2,1,0:T(1,128)S(1)}, u32[]{:S(2)}, u32[]{:S(2)}) collective-permute-start(f32[8,4,1,512]{3,2,1,0:T(1,128)S(1)} %get-tuple-element.275), channel_id=1, source_target_pairs={{0,1},{1,2},{2,3},{4,5},{5,6},{6,7},{8,9},{9,10},{10,11},{12,13},{... | collective-permute-start | bytes 196616 | tf_op jit(solution)/shard_map/ppermute | solution.py:46
  180.7 2.8 %collective-permute-done.32 = f32[8,4,1,512]{3,2,1,0:T(1,128)S(1)} collective-permute-done((f32[8,4,1,512]{3,2,1,0:T(1,128)S(1)}, f32[8,4,1,512]{3,2,1,0:T(1,128)S(1)}, u32[]{:S(2)}, u32[]{:S(2)}) %collective-permute-start.32) | collective-permute-done | bytes 65568 | tf_op jit(solution)/shard_map/ppermute | solution.py:46
  186.5 3.6 %collective-permute-done.33 = f32[1,8,128]{2,1,0:T(8,128)S(1)} collective-permute-done((f32[1,8,128]{2,1,0:T(8,128)S(1)}, f32[1,8,128]{2,1,0:T(8,128)S(1)}, u32[]{:S(2)}, u32[]{:S(2)}) %collective-permute-start.33) | collective-permute-done | bytes 4128 | tf_op jit(solution)/shard_map/ppermute | solution.py:31
  190.1 2.9 %collective-permute-start.34 = (f32[2,8,128]{2,1,0:T(8,128)S(1)}, f32[2,8,128]{2,1,0:T(8,128)S(1)}, u32[]{:S(2)}, u32[]{:S(2)}) collective-permute-start(f32[2,8,128]{2,1,0:T(8,128)S(1)} %get-tuple-element.326), channel_id=1, source_target_pairs={{0,8},{4,12},{8,0},{12,4},{16,24},{20,28},{24,16},{28,20},{1,9},{5... | collective-permute-start | bytes 24584 | tf_op jit(solution)/shard_map/ppermute | solution.py:31
  194.7 3.6 %collective-permute-start.35 = (f32[4,8,128]{2,1,0:T(8,128)S(1)}, f32[4,8,128]{2,1,0:T(8,128)S(1)}, u32[]{:S(2)}, u32[]{:S(2)}) collective-permute-start(f32[4,8,128]{2,1,0:T(8,128)S(1)} %bitcast.101), channel_id=1, source_target_pairs={{0,16},{4,20},{8,24},{12,28},{16,0},{20,4},{24,8},{28,12},{1,17},{... | collective-permute-start | bytes 49160 | tf_op jit(solution)/shard_map/ppermute | solution.py:31
  200.6 27.7 %gather_fusion.2 = f32[8192,8]{1,0:T(8,128)} fusion(f32[8,128]{0,1:T(8,128)S(1)} %copy.15, s32[8192]{0:T(1024)S(1)} %fusion.122), kind=kCustom, calls=%fused_computation.1.clone | custom fusion | bytes 557056 | tf_op jit(solution)/shard_map/jit(_take)/gather | solution.py:179
  228.3 7.4 %broadcast_select_fusion = f32[8192,8]{1,0:T(8,128)} fusion(f32[8192,8]{1,0:T(8,128)} %gather_fusion.2, pred[8192]{0:T(1024)(128)(4,1)S(1)} %compare_and_fusion), kind=kLoop, calls=%fused_computation.15 | loop fusion | flops 65536 | bytes 532480 | tf_op jit(solution)/shard_map/jit(_take)/select_n | solution.py:179
  235.7 2.8 %copy.16 = f32[8,2,8,512]{3,2,1,0:T(8,128)S(1)} copy(f32[8,2,8,512]{0,3,2,1:T(8,128)} %bitcast.92) | data formatting | bytes 524288 | tf_op jit(solution)/shard_map/reshape | solution.py:179
  238.6 3.3 %collective-permute-start.36 = (f32[8,1,8,512]{3,2,1,0:T(8,128)S(1)}, f32[8,1,8,512]{3,2,1,0:T(8,128)S(1)}, u32[]{:S(2)}, u32[]{:S(2)}) collective-permute-start(f32[8,1,8,512]{3,2,1,0:T(8,128)S(1)} %get-tuple-element.294), channel_id=1, source_target_pairs={{4,0},{8,4},{12,8},{16,12},{20,16},{24,20},{28,24},{5,1},{9,5},{13... | collective-permute-start | bytes 393224 | tf_op jit(solution)/shard_map/ppermute | solution.py:48
  241.9 3.5 %collective-permute-start.37 = (f32[8,1,8,512]{3,2,1,0:T(8,128)S(1)}, f32[8,1,8,512]{3,2,1,0:T(8,128)S(1)}, u32[]{:S(2)}, u32[]{:S(2)}) collective-permute-start(f32[8,1,8,512]{3,2,1,0:T(8,128)S(1)} %get-tuple-element.293), channel_id=1, source_target_pairs={{0,4},{4,8},{8,12},{12,16},{16,20},{20,24},{24,28},{1,5},{5,9},{9,... | collective-permute-start | bytes 393224 | tf_op jit(solution)/shard_map/ppermute | solution.py:46
  253.3 3.0 %collective-permute-done.39 = f32[8,4,1,512]{3,2,1,0:T(1,128)S(1)} collective-permute-done((f32[8,4,1,512]{3,2,1,0:T(1,128)S(1)}, f32[8,4,1,512]{3,2,1,0:T(1,128)S(1)}, u32[]{:S(2)}, u32[]{:S(2)}) %collective-permute-start.39) | collective-permute-done | bytes 65568 | tf_op jit(solution)/shard_map/ppermute | solution.py:46
  (155 shorter events, 94.9 us)
Async XLA Ops:
  0.0 16.2 %collective-permute-start.2 = (f32[8,1,8,512]{3,2,1,0:T(8,128)S(1)}, f32[8,1,8,512]{3,2,1,0:T(8,128)S(1)}, u32[]{:S(2)}, u32[]{:S(2)}) collective-permute-start(f32[8,1,8,512]{3,2,1,0:T(8,128)S(1)} %broadcast.145), channel_id=1, source_target_pairs={{4,0},{8,4},{12,8},{16,12},{20,16},{24,20},{28,24},{5,1},{9,5},{13... | collective-permute-start | bytes 393224 | tf_op jit(solution)/shard_map/ppermute | solution.py:48
  2.6 13.6 %collective-permute-start.3 = (f32[8,1,8,512]{3,2,1,0:T(8,128)S(1)}, f32[8,1,8,512]{3,2,1,0:T(8,128)S(1)}, u32[]{:S(2)}, u32[]{:S(2)}) collective-permute-start(f32[8,1,8,512]{3,2,1,0:T(8,128)S(1)} %broadcast.145), channel_id=1, source_target_pairs={{0,4},{4,8},{8,12},{12,16},{16,20},{20,24},{24,28},{1,5},{5,9},{9,... | collective-permute-start | bytes 393224 | tf_op jit(solution)/shard_map/ppermute | solution.py:46
  7.6 6.3 %collective-permute-start = (s32[1,8,512]{2,1,0:T(8,128)S(1)}, s32[1,8,512]{2,1,0:T(8,128)S(1)}, u32[]{:S(2)}, u32[]{:S(2)}) collective-permute-start(s32[1,8,512]{2,1,0:T(8,128)S(1)} %slice_bitcast_fusion.4), channel_id=1, source_target_pairs={{0,4},{4,8},{8,12},{12,16},{16,20},{20,24},{24,28},{1,5},{5,9},{9,... | collective-permute-start | bytes 49160 | tf_op jit(solution)/shard_map/ppermute | solution.py:58
  10.9 4.9 %collective-permute-start.1 = (s32[2,1,512]{2,1,0:T(1,128)S(1)}, s32[2,1,512]{2,1,0:T(1,128)S(1)}, u32[]{:S(2)}, u32[]{:S(2)}) collective-permute-start(s32[2,1,512]{2,1,0:T(1,128)S(1)} %slice_bitcast_fusion.5), channel_id=1, source_target_pairs={{0,1},{1,2},{2,3},{4,5},{5,6},{6,7},{8,9},{9,10},{10,11},{12,13},{... | collective-permute-start | bytes 12296 | tf_op jit(solution)/shard_map/ppermute | solution.py:58
  18.3 5.6 %collective-permute-start.5 = (f32[8,4,1,512]{3,2,1,0:T(1,128)S(1)}, f32[8,4,1,512]{3,2,1,0:T(1,128)S(1)}, u32[]{:S(2)}, u32[]{:S(2)}) collective-permute-start(f32[8,4,1,512]{3,2,1,0:T(1,128)S(1)} %get-tuple-element.287), channel_id=1, source_target_pairs={{0,1},{1,2},{2,3},{4,5},{5,6},{6,7},{8,9},{9,10},{10,11},{12,13},{... | collective-permute-start | bytes 196616 | tf_op jit(solution)/shard_map/ppermute | solution.py:46
  24.2 7.9 %collective-permute-start.6 = (f32[8,1,8,512]{3,2,1,0:T(8,128)S(1)}, f32[8,1,8,512]{3,2,1,0:T(8,128)S(1)}, u32[]{:S(2)}, u32[]{:S(2)}) collective-permute-start(f32[8,1,8,512]{3,2,1,0:T(8,128)S(1)} %get-tuple-element.318), channel_id=1, source_target_pairs={{4,0},{8,4},{12,8},{16,12},{20,16},{24,20},{28,24},{5,1},{9,5},{13... | collective-permute-start | bytes 393224 | tf_op jit(solution)/shard_map/ppermute | solution.py:48
  27.4 6.9 %collective-permute-start.7 = (f32[8,1,8,512]{3,2,1,0:T(8,128)S(1)}, f32[8,1,8,512]{3,2,1,0:T(8,128)S(1)}, u32[]{:S(2)}, u32[]{:S(2)}) collective-permute-start(f32[8,1,8,512]{3,2,1,0:T(8,128)S(1)} %get-tuple-element.317), channel_id=1, source_target_pairs={{0,4},{4,8},{8,12},{12,16},{16,20},{20,24},{24,28},{1,5},{5,9},{9,... | collective-permute-start | bytes 393224 | tf_op jit(solution)/shard_map/ppermute | solution.py:46
  36.3 5.6 %collective-permute-start.9 = (f32[8,4,1,512]{3,2,1,0:T(1,128)S(1)}, f32[8,4,1,512]{3,2,1,0:T(1,128)S(1)}, u32[]{:S(2)}, u32[]{:S(2)}) collective-permute-start(f32[8,4,1,512]{3,2,1,0:T(1,128)S(1)} %get-tuple-element.285), channel_id=1, source_target_pairs={{0,1},{1,2},{2,3},{4,5},{5,6},{6,7},{8,9},{9,10},{10,11},{12,13},{... | collective-permute-start | bytes 196616 | tf_op jit(solution)/shard_map/ppermute | solution.py:46
  42.2 8.1 %collective-permute-start.10 = (f32[8,1,8,512]{3,2,1,0:T(8,128)S(1)}, f32[8,1,8,512]{3,2,1,0:T(8,128)S(1)}, u32[]{:S(2)}, u32[]{:S(2)}) collective-permute-start(f32[8,1,8,512]{3,2,1,0:T(8,128)S(1)} %get-tuple-element.314), channel_id=1, source_target_pairs={{4,0},{8,4},{12,8},{16,12},{20,16},{24,20},{28,24},{5,1},{9,5},{13... | collective-permute-start | bytes 393224 | tf_op jit(solution)/shard_map/ppermute | solution.py:48
  44.1 7.3 %collective-permute-start.11 = (f32[8,1,8,512]{3,2,1,0:T(8,128)S(1)}, f32[8,1,8,512]{3,2,1,0:T(8,128)S(1)}, u32[]{:S(2)}, u32[]{:S(2)}) collective-permute-start(f32[8,1,8,512]{3,2,1,0:T(8,128)S(1)} %get-tuple-element.313), channel_id=1, source_target_pairs={{0,4},{4,8},{8,12},{12,16},{16,20},{20,24},{24,28},{1,5},{5,9},{9,... | collective-permute-start | bytes 393224 | tf_op jit(solution)/shard_map/ppermute | solution.py:46
  53.5 5.6 %collective-permute-start.13 = (f32[8,4,1,512]{3,2,1,0:T(1,128)S(1)}, f32[8,4,1,512]{3,2,1,0:T(1,128)S(1)}, u32[]{:S(2)}, u32[]{:S(2)}) collective-permute-start(f32[8,4,1,512]{3,2,1,0:T(1,128)S(1)} %get-tuple-element.283), channel_id=1, source_target_pairs={{0,1},{1,2},{2,3},{4,5},{5,6},{6,7},{8,9},{9,10},{10,11},{12,13},{... | collective-permute-start | bytes 196616 | tf_op jit(solution)/shard_map/ppermute | solution.py:46
  69.9 4.8 %collective-permute-start.16 = (f32[4,8,128]{2,1,0:T(8,128)S(1)}, f32[4,8,128]{2,1,0:T(8,128)S(1)}, u32[]{:S(2)}, u32[]{:S(2)}) collective-permute-start(f32[4,8,128]{2,1,0:T(8,128)S(1)} %bitcast.99), channel_id=1, source_target_pairs={{0,16},{4,20},{8,24},{12,28},{16,0},{20,4},{24,8},{28,12},{1,17},{... | collective-permute-start | bytes 49160 | tf_op jit(solution)/shard_map/ppermute | solution.py:31
  113.3 7.8 %collective-permute-start.17 = (f32[8,1,8,512]{3,2,1,0:T(8,128)S(1)}, f32[8,1,8,512]{3,2,1,0:T(8,128)S(1)}, u32[]{:S(2)}, u32[]{:S(2)}) collective-permute-start(f32[8,1,8,512]{3,2,1,0:T(8,128)S(1)} %get-tuple-element.310), channel_id=1, source_target_pairs={{4,0},{8,4},{12,8},{16,12},{20,16},{24,20},{28,24},{5,1},{9,5},{13... | collective-permute-start | bytes 393224 | tf_op jit(solution)/shard_map/ppermute | solution.py:48
  116.6 6.9 %collective-permute-start.18 = (f32[8,1,8,512]{3,2,1,0:T(8,128)S(1)}, f32[8,1,8,512]{3,2,1,0:T(8,128)S(1)}, u32[]{:S(2)}, u32[]{:S(2)}) collective-permute-start(f32[8,1,8,512]{3,2,1,0:T(8,128)S(1)} %get-tuple-element.309), channel_id=1, source_target_pairs={{0,4},{4,8},{8,12},{12,16},{16,20},{20,24},{24,28},{1,5},{5,9},{9,... | collective-permute-start | bytes 393224 | tf_op jit(solution)/shard_map/ppermute | solution.py:46
  125.5 5.6 %collective-permute-start.20 = (f32[8,4,1,512]{3,2,1,0:T(1,128)S(1)}, f32[8,4,1,512]{3,2,1,0:T(1,128)S(1)}, u32[]{:S(2)}, u32[]{:S(2)}) collective-permute-start(f32[8,4,1,512]{3,2,1,0:T(1,128)S(1)} %get-tuple-element.281), channel_id=1, source_target_pairs={{0,1},{1,2},{2,3},{4,5},{5,6},{6,7},{8,9},{9,10},{10,11},{12,13},{... | collective-permute-start | bytes 196616 | tf_op jit(solution)/shard_map/ppermute | solution.py:46
  131.4 7.8 %collective-permute-start.21 = (f32[8,1,8,512]{3,2,1,0:T(8,128)S(1)}, f32[8,1,8,512]{3,2,1,0:T(8,128)S(1)}, u32[]{:S(2)}, u32[]{:S(2)}) collective-permute-start(f32[8,1,8,512]{3,2,1,0:T(8,128)S(1)} %get-tuple-element.306), channel_id=1, source_target_pairs={{4,0},{8,4},{12,8},{16,12},{20,16},{24,20},{28,24},{5,1},{9,5},{13... | collective-permute-start | bytes 393224 | tf_op jit(solution)/shard_map/ppermute | solution.py:48
  133.3 7.3 %collective-permute-start.22 = (f32[8,1,8,512]{3,2,1,0:T(8,128)S(1)}, f32[8,1,8,512]{3,2,1,0:T(8,128)S(1)}, u32[]{:S(2)}, u32[]{:S(2)}) collective-permute-start(f32[8,1,8,512]{3,2,1,0:T(8,128)S(1)} %get-tuple-element.305), channel_id=1, source_target_pairs={{0,4},{4,8},{8,12},{12,16},{16,20},{20,24},{24,28},{1,5},{5,9},{9,... | collective-permute-start | bytes 393224 | tf_op jit(solution)/shard_map/ppermute | solution.py:46
  140.7 4.5 %collective-permute-start.23 = (f32[8,4,1,512]{3,2,1,0:T(1,128)S(1)}, f32[8,4,1,512]{3,2,1,0:T(1,128)S(1)}, u32[]{:S(2)}, u32[]{:S(2)}) collective-permute-start(f32[8,4,1,512]{3,2,1,0:T(1,128)S(1)} %get-tuple-element.278), channel_id=1, source_target_pairs={{1,0},{2,1},{3,2},{5,4},{6,5},{7,6},{9,8},{10,9},{11,10},{13,12},{... | collective-permute-start | bytes 196616 | tf_op jit(solution)/shard_map/ppermute | solution.py:48
  142.6 5.6 %collective-permute-start.24 = (f32[8,4,1,512]{3,2,1,0:T(1,128)S(1)}, f32[8,4,1,512]{3,2,1,0:T(1,128)S(1)}, u32[]{:S(2)}, u32[]{:S(2)}) collective-permute-start(f32[8,4,1,512]{3,2,1,0:T(1,128)S(1)} %get-tuple-element.279), channel_id=1, source_target_pairs={{0,1},{1,2},{2,3},{4,5},{5,6},{6,7},{8,9},{9,10},{10,11},{12,13},{... | collective-permute-start | bytes 196616 | tf_op jit(solution)/shard_map/ppermute | solution.py:46
  148.5 8.3 %collective-permute-start.25 = (f32[8,1,8,512]{3,2,1,0:T(8,128)S(1)}, f32[8,1,8,512]{3,2,1,0:T(8,128)S(1)}, u32[]{:S(2)}, u32[]{:S(2)}) collective-permute-start(f32[8,1,8,512]{3,2,1,0:T(8,128)S(1)} %get-tuple-element.302), channel_id=1, source_target_pairs={{4,0},{8,4},{12,8},{16,12},{20,16},{24,20},{28,24},{5,1},{9,5},{13... | collective-permute-start | bytes 393224 | tf_op jit(solution)/shard_map/ppermute | solution.py:48
  150.5 7.8 %collective-permute-start.26 = (f32[8,1,8,512]{3,2,1,0:T(8,128)S(1)}, f32[8,1,8,512]{3,2,1,0:T(8,128)S(1)}, u32[]{:S(2)}, u32[]{:S(2)}) collective-permute-start(f32[8,1,8,512]{3,2,1,0:T(8,128)S(1)} %get-tuple-element.301), channel_id=1, source_target_pairs={{0,4},{4,8},{8,12},{12,16},{16,20},{20,24},{24,28},{1,5},{5,9},{9,... | collective-permute-start | bytes 393224 | tf_op jit(solution)/shard_map/ppermute | solution.py:46
  158.4 4.5 %collective-permute-start.27 = (f32[8,4,1,512]{3,2,1,0:T(1,128)S(1)}, f32[8,4,1,512]{3,2,1,0:T(1,128)S(1)}, u32[]{:S(2)}, u32[]{:S(2)}) collective-permute-start(f32[8,4,1,512]{3,2,1,0:T(1,128)S(1)} %get-tuple-element.276), channel_id=1, source_target_pairs={{1,0},{2,1},{3,2},{5,4},{6,5},{7,6},{9,8},{10,9},{11,10},{13,12},{... | collective-permute-start | bytes 196616 | tf_op jit(solution)/shard_map/ppermute | solution.py:48
  160.3 5.6 %collective-permute-start.28 = (f32[8,4,1,512]{3,2,1,0:T(1,128)S(1)}, f32[8,4,1,512]{3,2,1,0:T(1,128)S(1)}, u32[]{:S(2)}, u32[]{:S(2)}) collective-permute-start(f32[8,4,1,512]{3,2,1,0:T(1,128)S(1)} %get-tuple-element.277), channel_id=1, source_target_pairs={{0,1},{1,2},{2,3},{4,5},{5,6},{6,7},{8,9},{9,10},{10,11},{12,13},{... | collective-permute-start | bytes 196616 | tf_op jit(solution)/shard_map/ppermute | solution.py:46
  166.2 8.2 %collective-permute-start.29 = (f32[8,1,8,512]{3,2,1,0:T(8,128)S(1)}, f32[8,1,8,512]{3,2,1,0:T(8,128)S(1)}, u32[]{:S(2)}, u32[]{:S(2)}) collective-permute-start(f32[8,1,8,512]{3,2,1,0:T(8,128)S(1)} %get-tuple-element.298), channel_id=1, source_target_pairs={{4,0},{8,4},{12,8},{16,12},{20,16},{24,20},{28,24},{5,1},{9,5},{13... | collective-permute-start | bytes 393224 | tf_op jit(solution)/shard_map/ppermute | solution.py:48
  168.1 7.8 %collective-permute-start.30 = (f32[8,1,8,512]{3,2,1,0:T(8,128)S(1)}, f32[8,1,8,512]{3,2,1,0:T(8,128)S(1)}, u32[]{:S(2)}, u32[]{:S(2)}) collective-permute-start(f32[8,1,8,512]{3,2,1,0:T(8,128)S(1)} %get-tuple-element.297), channel_id=1, source_target_pairs={{0,4},{4,8},{8,12},{12,16},{16,20},{20,24},{24,28},{1,5},{5,9},{9,... | collective-permute-start | bytes 393224 | tf_op jit(solution)/shard_map/ppermute | solution.py:46
  176.0 4.7 %collective-permute-start.31 = (f32[8,4,1,512]{3,2,1,0:T(1,128)S(1)}, f32[8,4,1,512]{3,2,1,0:T(1,128)S(1)}, u32[]{:S(2)}, u32[]{:S(2)}) collective-permute-start(f32[8,4,1,512]{3,2,1,0:T(1,128)S(1)} %get-tuple-element.274), channel_id=1, source_target_pairs={{1,0},{2,1},{3,2},{5,4},{6,5},{7,6},{9,8},{10,9},{11,10},{13,12},{... | collective-permute-start | bytes 196616 | tf_op jit(solution)/shard_map/ppermute | solution.py:48
  177.9 5.6 %collective-permute-start.32 = (f32[8,4,1,512]{3,2,1,0:T(1,128)S(1)}, f32[8,4,1,512]{3,2,1,0:T(1,128)S(1)}, u32[]{:S(2)}, u32[]{:S(2)}) collective-permute-start(f32[8,4,1,512]{3,2,1,0:T(1,128)S(1)} %get-tuple-element.275), channel_id=1, source_target_pairs={{0,1},{1,2},{2,3},{4,5},{5,6},{6,7},{8,9},{9,10},{10,11},{12,13},{... | collective-permute-start | bytes 196616 | tf_op jit(solution)/shard_map/ppermute | solution.py:46
  190.1 4.5 %collective-permute-start.34 = (f32[2,8,128]{2,1,0:T(8,128)S(1)}, f32[2,8,128]{2,1,0:T(8,128)S(1)}, u32[]{:S(2)}, u32[]{:S(2)}) collective-permute-start(f32[2,8,128]{2,1,0:T(8,128)S(1)} %get-tuple-element.326), channel_id=1, source_target_pairs={{0,8},{4,12},{8,0},{12,4},{16,24},{20,28},{24,16},{28,20},{1,9},{5... | collective-permute-start | bytes 24584 | tf_op jit(solution)/shard_map/ppermute | solution.py:31
  194.7 5.3 %collective-permute-start.35 = (f32[4,8,128]{2,1,0:T(8,128)S(1)}, f32[4,8,128]{2,1,0:T(8,128)S(1)}, u32[]{:S(2)}, u32[]{:S(2)}) collective-permute-start(f32[4,8,128]{2,1,0:T(8,128)S(1)} %bitcast.101), channel_id=1, source_target_pairs={{0,16},{4,20},{8,24},{12,28},{16,0},{20,4},{24,8},{28,12},{1,17},{... | collective-permute-start | bytes 49160 | tf_op jit(solution)/shard_map/ppermute | solution.py:31
  238.6 7.8 %collective-permute-start.36 = (f32[8,1,8,512]{3,2,1,0:T(8,128)S(1)}, f32[8,1,8,512]{3,2,1,0:T(8,128)S(1)}, u32[]{:S(2)}, u32[]{:S(2)}) collective-permute-start(f32[8,1,8,512]{3,2,1,0:T(8,128)S(1)} %get-tuple-element.294), channel_id=1, source_target_pairs={{4,0},{8,4},{12,8},{16,12},{20,16},{24,20},{28,24},{5,1},{9,5},{13... | collective-permute-start | bytes 393224 | tf_op jit(solution)/shard_map/ppermute | solution.py:48
  241.9 6.9 %collective-permute-start.37 = (f32[8,1,8,512]{3,2,1,0:T(8,128)S(1)}, f32[8,1,8,512]{3,2,1,0:T(8,128)S(1)}, u32[]{:S(2)}, u32[]{:S(2)}) collective-permute-start(f32[8,1,8,512]{3,2,1,0:T(8,128)S(1)} %get-tuple-element.293), channel_id=1, source_target_pairs={{0,4},{4,8},{8,12},{12,16},{16,20},{20,24},{24,28},{1,5},{5,9},{9,... | collective-permute-start | bytes 393224 | tf_op jit(solution)/shard_map/ppermute | solution.py:46
  250.8 5.6 %collective-permute-start.39 = (f32[8,4,1,512]{3,2,1,0:T(1,128)S(1)}, f32[8,4,1,512]{3,2,1,0:T(1,128)S(1)}, u32[]{:S(2)}, u32[]{:S(2)}) collective-permute-start(f32[8,4,1,512]{3,2,1,0:T(1,128)S(1)} %get-tuple-element.273), channel_id=1, source_target_pairs={{0,1},{1,2},{2,3},{4,5},{5,6},{6,7},{8,9},{9,10},{10,11},{12,13},{... | collective-permute-start | bytes 196616 | tf_op jit(solution)/shard_map/ppermute | solution.py:46
  (10 other events, 115.9 us)
